TPU v7x, 256 devices: a whole 4x4x8 slice. The times are simulated.
256 devices in a mesh: batch: 64 (over y, z, core), feat: 4 (over x).
Axes of the slice: x: 4, y: 4, z: 8, core: 2. Of those that a mesh axis runs over, the one named last changes fastest.
Arguments:
- tables: bfloat16 [4, 128, 2048, 192], P('feat', 'batch'), may hold values from -3 to 3
- bag_ids: int32 [4, 128, 4, 8192], P('feat', 'batch'), may hold values from 0 to 2047
- bag_lengths: int32 [4, 128, 8192], P('feat', 'batch'), may hold values from 1 to 4
- pair_groups: int32 [16, 2], replicated, may hold values from 0 to 15
- compress: bfloat16 [16, 32, 8], P('feat'), may hold values from -1 to 1
- w_hidden: bfloat16 [16, 32, 8, 4096], P('feat'), may hold values from -0.09375 to 0.09375
- hidden_bias: float32 [4096], replicated, may hold values from -4 to 4
- norm_gain: float32 [4096], P('feat'), may hold values from 0.1 to 1.9
Outputs:
- interacted: bfloat16 [8192, 4096], P('batch', 'feat')
Inputs may be any that keep to these rules, and one draw needn't show every extreme that they name: `bag_lengths`: ids at slots from a bag's length on are ignored.
All inputs are finite; a program needn't handle non-finite values.
Results may differ from a plain program's by a relative error of at most 0.0052.
Values may be sent and summed in bfloat16 or wider, within the bound.
A program may use at most 128 MiB of HBM per device.

v0:
```python
import jax
import jax.numpy as jnp
from jax import lax
from jax.sharding import PartitionSpec as P


def take_rows(table_one, ids_one):
    return jnp.take(table_one, ids_one, axis=0)


def select_groups(source, pair_list, group_size):
    offsets = jnp.arange(group_size, dtype=jnp.int32)
    wanted = pair_list[:, :, None] * group_size + offsets[None, None, :]
    shape_out = (pair_list.shape[0], 2, group_size, source.shape[1], source.shape[2])
    return jnp.take(source, wanted.reshape(-1), axis=0).reshape(shape_out)


def squeeze_pairs(chosen, weights):
    row_blocks = chosen[:, 0]
    col_blocks = chosen[:, 1]
    gram_scale = float(chosen.shape[4]) ** (-0.5)
    gram_blocks = (
        jnp.einsum("qfbd,qgbd->qbfg", row_blocks, col_blocks, preferred_element_type=jnp.float32)
        * gram_scale
    )
    squeezed = jnp.einsum(
        "qbfg,qgk->bqfk", gram_blocks, weights.astype(jnp.float32), precision=lax.Precision.HIGHEST
    )
    return squeezed.astype(jnp.bfloat16)


def body(tables, bag_ids, bag_lengths, pair_groups, compress, w_hidden, hidden_bias, norm_gain):
    own_tables = tables[0]
    own_ids = bag_ids[0]
    own_lengths = bag_lengths[0]
    slot_count = own_ids.shape[1]
    pooled_sum = jnp.zeros((own_ids.shape[0], own_ids.shape[2], own_tables.shape[2]), jnp.float32)
    for slot in range(slot_count):
        looked = jax.vmap(take_rows)(own_tables, own_ids[:, slot, :])
        live = (own_lengths > slot)[:, :, None]
        pooled_sum = pooled_sum + jnp.where(live, looked.astype(jnp.float32), 0.0)
    pooled = pooled_sum.astype(jnp.bfloat16)
    feature_tile = lax.all_to_all(pooled, "batch", split_axis=1, concat_axis=0, tiled=True)
    samples = feature_tile.shape[1]
    pair_count = compress.shape[0]
    group_size = compress.shape[1]
    first_pair = lax.axis_index("feat") * pair_count
    local_pairs = lax.dynamic_slice_in_dim(pair_groups, first_pair, pair_count, 0)
    everything = lax.all_gather(feature_tile, "feat", axis=0, tiled=True)
    squeezed = squeeze_pairs(select_groups(everything, local_pairs, group_size), compress)
    squeezed = squeezed.reshape(samples, -1)
    w_flat = w_hidden.reshape(-1, w_hidden.shape[3])
    hid_local = norm_gain.shape[0]
    hid_total = hid_local * lax.axis_size("feat")
    own_start = lax.axis_index("feat") * hid_local
    hidden = lax.psum_scatter(
        lax.dot_general(
            w_flat, squeezed, (((0,), (1,)), ((), ())), preferred_element_type=jnp.float32
        ),
        "feat",
        scatter_dimension=0,
        tiled=True,
    )
    local_bias = lax.dynamic_slice_in_dim(hidden_bias, own_start, hid_local, 0)
    hidden = hidden + local_bias[:, None]
    row_sum, row_squares = lax.psum(
        (jnp.sum(hidden, axis=0), jnp.sum(hidden * hidden, axis=0)), "feat"
    )
    row_mean = row_sum / hid_total
    spread = row_squares / hid_total - row_mean * row_mean
    normed = (hidden - row_mean[None, :]) * lax.rsqrt(spread + 1e-05)[None, :] * norm_gain[:, None]
    return jax.nn.silu(normed).T.astype(jnp.bfloat16)


def solution(mesh):
    in_specs = (
        P("feat", "batch", None, None),
        P("feat", "batch", None, None),
        P("feat", "batch", None),
        P(),
        P("feat", None, None),
        P("feat", None, None, None),
        P(),
        P("feat"),
    )
    out_specs = P("batch", "feat")
    return jax.shard_map(body, mesh=mesh, in_specs=in_specs, out_specs=out_specs, check_vma=False)
```

profile of v0, /device:TPU:8, one launch (start us, length us, event | category | flops | bytes accessed | tf_op | source)
XLA Modules:
  0.0 1334.6 jit_solution(744671372483452733)
XLA Ops:
  6.5 1.8 fusion.15
  9.1 2.7 copy.38
  11.9 161.2 %gather_fusion.3 = bf16[16384,192]{1,0:T(8,128)(2,1)} fusion(bf16[2,2048,192]{2,1,0:T(8,128)(2,1)S(1)} %bitcast.104, s32[16384]{0:T(1024)S(1)} %bitcast.108), kind=kCustom, calls=%fused_computation.2.clone | custom fusion | bytes 12713984 | tf_op jit(solution)/shard_map/vmap(jit(_take))/gather | solution.py:8
  173.1 161.2 %gather_fusion.4 = bf16[16384,192]{1,0:T(8,128)(2,1)} fusion(bf16[2,2048,192]{2,1,0:T(8,128)(2,1)S(1)} %bitcast.105, s32[16384]{0:T(1024)S(1)} %bitcast.109), kind=kCustom, calls=%fused_computation.3.clone | custom fusion | bytes 12713984 | tf_op jit(solution)/shard_map/vmap(jit(_take))/gather | solution.py:8
  334.3 161.1 %gather_fusion.1 = bf16[16384,192]{1,0:T(8,128)(2,1)} fusion(bf16[2,2048,192]{2,1,0:T(8,128)(2,1)S(1)} %bitcast.106, s32[16384]{0:T(1024)S(1)} %bitcast.111), kind=kCustom, calls=%fused_computation.clone | custom fusion | bytes 12713984 | tf_op jit(solution)/shard_map/vmap(jit(_take))/gather | solution.py:8
  495.4 161.2 %gather_fusion.2 = bf16[16384,192]{1,0:T(8,128)(2,1)} fusion(bf16[2,2048,192]{2,1,0:T(8,128)(2,1)S(1)} %bitcast.107, s32[16384]{0:T(1024)S(1)} %bitcast.110), kind=kCustom, calls=%fused_computation.1.clone | custom fusion | bytes 12713984 | tf_op jit(solution)/shard_map/vmap(jit(_take))/gather | solution.py:8
  661.8 2.2 copy.47
  664.2 2.2 copy.36
  666.3 2.1 copy.40
  668.5 2.1 copy.43
  670.6 2.2 copy.46
  672.8 79.1 %add_convert_fusion = bf16[2,8192,192]{2,0,1:T(2,128)(2,1)S(1)} fusion(pred[2,8192]{0,1:T(8,128)(4,1)} %copy.46, pred[2,8192]{0,1:T(8,128)(4,1)} %copy.43, pred[2,8192]{0,1:T(8,128)(4,1)} %copy.40, pred[2,8192]{0,1:T(8,128)(4,1)} %copy.36, pred[2,8192]{0,1:T(8,128)(4,1)S(1)} %copy.37, pred[2,8192]{0,1:T(8,128)(4,1)S(1)} %copy.41, ...), kind=kLoop, calls=%fused_computation.5 | loop fusion | flops 50331648 | bytes 31588352 | tf_op jit(solution)/shard_map/convert_element_type | solution.py:42
  751.8 196.1 %all_to_all.18 = bf16[2,8192,192]{2,0,1:T(2,128)(2,1)} all-to-all(bf16[2,8192,192]{2,0,1:T(2,128)(2,1)S(1)} %add_convert_fusion), channel_id=1, replica_groups=mesh['batch'=64,'feat'=4] {'batch'}, dimensions={1} | all-to-all | bytes 12582912 | tf_op jit(solution)/shard_map/all_to_all | solution.py:43
  948.0 20.4 %copy.56 = bf16[2,64,128,192]{2,3,0,1:T(8,128)(2,1)} copy(bf16[2,64,128,192]{3,0,2,1:T(2,128)(2,1)} %bitcast.113) | data formatting | bytes 12582912 | tf_op jit(solution)/shard_map/all_to_all | solution.py:43
  969.1 224.3 %all-gather.2.cloned.1.call-done = bf16[512,128,192]{1,2,0:T(8,128)(2,1)} async-done(((bf16[128,128,192]{1,2,0:T(8,128)(2,1)}), bf16[512,128,192]{1,2,0:T(8,128)(2,1)}) %all-gather.2.cloned.1.call-update) | async-done | bytes 25165840 | tf_op jit(solution)/shard_map/all_gather | solution.py:49
  1193.3 18.8 %gather_fusion = bf16[256,128,192]{1,2,0:T(8,128)(2,1)} fusion(bf16[512,128,192]{1,2,0:T(8,128)(2,1)} %all-gather.2.cloned.1.call-done, s32[1024]{0:T(1024)S(1)} %pad_clamp_fusion), kind=kCustom, calls=%fused_computation.4 | custom fusion | bytes 25166848 | tf_op jit(solution)/shard_map/jit(_take)/gather | solution.py:15
  1212.1 27.1 %copy.51 = bf16[4,2,32,128,192]{4,2,3,0,1:T(8,128)(2,1)} copy(bf16[4,2,32,128,192]{3,4,2,1,0:T(8,128)(2,1)} %bitcast.112) | data formatting | bytes 25165824 | tf_op jit(solution)/shard_map/jit(_take)/gather | solution.py:15
  1239.3 14.1 %broadcast_select_fusion.4 = bf16[4,2,32,128,192]{4,2,3,0,1:T(8,128)(2,1)} fusion(bf16[4,2,32,128,192]{4,2,3,0,1:T(8,128)(2,1)} %copy.51, pred[4,2,32]{2,0,1:T(4,128)(4,1)S(1)} %copy.35), kind=kLoop, calls=%fused_computation.10 | loop fusion | flops 6291456 | bytes 25166080 | tf_op jit(solution)/shard_map/jit(_take)/select_n | solution.py:15
  1253.4 11.3 broadcast_multiply_fusion
  1264.7 11.9 fusion.6
  1276.6 6.1 convolution_bitcast_fusion
  1283.4 32.5 %reduce-scatter.2.cloned.1.call-done = f32[1024,128]{0,1:T(8,128)} async-done(((f32[4096,128]{0,1:T(8,128)}), f32[1024,128]{0,1:T(8,128)}) %reduce-scatter.2.cloned.1.call-update) | async-done | bytes 524304 | tf_op jit(solution)/shard_map/reduce_scatter | solution.py:56
  1317.1 8.6 all-reduce
  1325.7 2.0 fusion.9
  (35 shorter events, 8.7 us)
Async XLA Ops:
  6.5 1258.2 %copy-start = (bf16[4,32,8]{1,2,0:T(8,128)(2,1)S(1)}, bf16[4,32,8]{1,2,0:T(8,128)(2,1)}, u32[]{:S(2)}) copy-start(bf16[4,32,8]{1,2,0:T(8,128)(2,1)} %param.14) | copy-start | bytes 6148
  6.5 1186.8 %all-gather.2.cloned.1.call-start = ((), (), s32[]{:S(2)}) async-start(), calls=%async_computation.2 | async-start | bytes 31457280 | tf_op jit(solution)/shard_map/all_gather | solution.py:49
  495.4 168.6 %copy-start.1 = (s32[1,2,8192]{2,1,0:T(2,128)S(1)}, s32[1,2,8192]{2,1,0:T(2,128)}, u32[]{:S(2)}) copy-start(s32[1,2,8192]{2,1,0:T(2,128)} %param.12) | copy-start | bytes 196612
  948.0 20.6 %copy-start.3 = (s32[16,2]{0,1:T(2,128)S(1)}, s32[16,2]{0,1:T(2,128)}, u32[]{:S(2)}) copy-start(s32[16,2]{0,1:T(2,128)} %param.13) | copy-start | bytes 388
  968.4 347.6 %reduce-scatter.2.cloned.1.call-start = ((), (), s32[]{:S(2)}) async-start(), calls=%async_computation.3 | async-start | bytes 2621440 | tf_op jit(solution)/shard_map/reduce_scatter | solution.py:56
  1276.6 49.1 %copy-start.2 = (f32[1024]{0:T(1024)S(1)}, f32[1024]{0:T(1024)}, u32[]{:S(2)}) copy-start(f32[1024]{0:T(1024)} %param.17) | copy-start | bytes 12292
Sparse Core Ops, SparseCore 0:
  968.5 224.7 all-gather.1
  1282.8 33.0 reduce-scatter.1
where the time goes:
time: 1340 us; the launch traced here: 1330 us
  local copies, waits for them, and re-layouts  732 us (55%)
  waiting for transfers between devices  257 us (19%)
  blocking collectives  205 us (15%)
  other arithmetic  97.5 us (7%)
  matrix products  29.3 us (2%)
  between operations  13.6 us (1%)
    gather x4, local copies, waits for them, and re-layouts, take_rows(): return jnp.take(table_one, ids_one, axis=0)  645 us
    all_gather x1, waiting for transfers between devices, body(): everything = lax.all_gather(feature_tile, 'feat', axis=0, tiled=True)  224 us
    all_to_all x1, blocking collectives, body(): lax.all_to_all(pooled, 'batch', split_axis=1, concat_axis=0, tiled=True)  196 us
    convert_element_type x1, other arithmetic, body(): pooled = pooled_sum.astype(jnp.bfloat16)  79.1 us
    gather x2, local copies, waits for them, and re-layouts, select_groups(): return jnp.take(source, wanted.reshape(-1), axis=0).reshape(shape_out)  45.9 us
    reduce_scatter x1, waiting for transfers between devices, body(): lax.psum_scatter(lax.dot_general(w_flat, squeezed, (((0,), (1,)), ((), ()...  32.5 us
  transfers between devices with their start and end apart: 2, of which 2 were waited for; matrix products, arithmetic and copies ran while one was open for 0% of the time, Pallas kernels for 0%

commit v1 on v0

--- a/solution.py
+++ b/solution.py
@@ -2,6 +2,12 @@
 import jax.numpy as jnp
 from jax import lax
 from jax.sharding import PartitionSpec as P
+
+
+def swap_blocks(block, name, split, join):
+    parts = jnp.split(block, lax.axis_size(name), axis=split)
+    arrived = lax.all_to_all(jnp.stack(parts), name, 0, 0)
+    return jnp.concatenate(arrived, axis=join)
 
 
 def take_rows(table_one, ids_one):
@@ -40,7 +46,7 @@
         live = (own_lengths > slot)[:, :, None]
         pooled_sum = pooled_sum + jnp.where(live, looked.astype(jnp.float32), 0.0)
     pooled = pooled_sum.astype(jnp.bfloat16)
-    feature_tile = lax.all_to_all(pooled, "batch", split_axis=1, concat_axis=0, tiled=True)
+    feature_tile = swap_blocks(pooled, "batch", 1, 0)
     samples = feature_tile.shape[1]
     pair_count = compress.shape[0]
     group_size = compress.shape[1]

time: 1340 us -> 1230 us (0.918)
  other arithmetic: 97.5 us -> 30.3 us
  blocking collectives: 205 us -> 160 us
    convert_element_type x1, other arithmetic: 79.1 us -> 11.9 us  [body(): pooled = pooled_sum.astype(jnp.bfloat16)]
    all_to_all x1, blocking collectives: 196 us -> 151 us  [swap_blocks(): arrived = lax.all_to_all(jnp.stack(parts), name, 0, 0)]
    gather x4 -> x8, local copies, waits for them, and re-layouts: 645 us -> 685 us  [take_rows(): return jnp.take(table_one, ids_one, axis=0)]
    all_to_all x1 -> x0, local copies, waits for them, and re-layouts: 20.4 us -> none  [body(): lax.all_to_all(pooled, 'batch', split_axis=1, concat_axis=0, tiled=True)]
where the time goes in v1:
time: 1230 us
  local copies, waits for them, and re-layouts  740 us (60%)
  waiting for transfers between devices  256 us (21%)
  blocking collectives  160 us (13%)
  other arithmetic  30.3 us (2%)
  matrix products  29.3 us (2%)
  between operations  13.6 us (1%)
    gather x8, local copies, waits for them, and re-layouts, take_rows(): return jnp.take(table_one, ids_one, axis=0)  685 us
    all_gather x1, waiting for transfers between devices, body(): everything = lax.all_gather(feature_tile, 'feat', axis=0, tiled=True)  224 us
    all_to_all x1, blocking collectives, swap_blocks(): arrived = lax.all_to_all(jnp.stack(parts), name, 0, 0)  151 us
    gather x2, local copies, waits for them, and re-layouts, select_groups(): return jnp.take(source, wanted.reshape(-1), axis=0).reshape(shape_out)  45.9 us
    reduce_scatter x1, waiting for transfers between devices, body(): lax.psum_scatter(lax.dot_general(w_flat, squeezed, (((0,), (1,)), ((), ()...  32.5 us
  transfers between devices with their start and end apart: 2, of which 2 were waited for; matrix products, arithmetic and copies ran while one was open for 0% of the time, Pallas kernels for 0%

profile of v1, /device:TPU:8, one launch (start us, length us, event | category | flops | bytes accessed | tf_op | source)
XLA Modules:
  0.0 1229.5 jit_solution(1471222722055289580)
XLA Ops:
  6.5 1.8 fusion.15
  9.1 2.7 copy.29
  11.9 161.2 %gather_fusion.1 = bf16[16384,192]{1,0:T(8,128)(2,1)} fusion(bf16[2,2048,192]{2,1,0:T(8,128)(2,1)S(1)} %bitcast.356, s32[16384]{0:T(1024)S(1)} %bitcast.360), kind=kCustom, calls=%fused_computation.clone | custom fusion | bytes 12713984 | tf_op jit(solution)/shard_map/vmap(jit(_take))/gather | solution.py:14
  173.1 10.1 copy.30
  183.2 161.2 %gather_fusion.2 = bf16[16384,192]{1,0:T(8,128)(2,1)} fusion(bf16[2,2048,192]{2,1,0:T(8,128)(2,1)S(1)} %bitcast.357, s32[16384]{0:T(1024)S(1)} %bitcast.362), kind=kCustom, calls=%fused_computation.1.clone | custom fusion | bytes 12713984 | tf_op jit(solution)/shard_map/vmap(jit(_take))/gather | solution.py:14
  344.5 10.1 copy.31
  354.5 161.2 %gather_fusion.3 = bf16[16384,192]{1,0:T(8,128)(2,1)} fusion(bf16[2,2048,192]{2,1,0:T(8,128)(2,1)S(1)} %bitcast.358, s32[16384]{0:T(1024)S(1)} %bitcast.363), kind=kCustom, calls=%fused_computation.2.clone | custom fusion | bytes 12713984 | tf_op jit(solution)/shard_map/vmap(jit(_take))/gather | solution.py:14
  515.7 10.2 copy.32
  525.9 161.2 %gather_fusion.4 = bf16[16384,192]{1,0:T(8,128)(2,1)} fusion(bf16[2,2048,192]{2,1,0:T(8,128)(2,1)S(1)} %bitcast.359, s32[16384]{0:T(1024)S(1)} %bitcast.361), kind=kCustom, calls=%fused_computation.3.clone | custom fusion | bytes 12713984 | tf_op jit(solution)/shard_map/vmap(jit(_take))/gather | solution.py:14
  687.1 10.1 copy.33
  697.4 11.9 add_convert_fusion
  712.1 151.2 %all_to_all.5 = bf16[64,2,128,192]{2,3,1,0:T(8,128)(2,1)} all-to-all(bf16[64,2,128,192]{2,3,1,0:T(8,128)(2,1)S(1)} %constant_dynamic-update-slice_fusion), channel_id=1, replica_groups=mesh['batch'=64,'feat'=4] {'batch'}, dimensions={0} | all-to-all | bytes 12582912 | tf_op jit(solution)/shard_map/all_to_all | solution.py:9
  864.4 223.9 %all-gather.2.cloned.1.call-done = bf16[512,128,192]{1,2,0:T(8,128)(2,1)} async-done(((bf16[128,128,192]{1,2,0:T(8,128)(2,1)}), bf16[512,128,192]{1,2,0:T(8,128)(2,1)}) %all-gather.2.cloned.1.call-update) | async-done | bytes 25165840 | tf_op jit(solution)/shard_map/all_gather | solution.py:55
  1088.3 18.8 %gather_fusion = bf16[256,128,192]{1,2,0:T(8,128)(2,1)} fusion(bf16[512,128,192]{1,2,0:T(8,128)(2,1)} %all-gather.2.cloned.1.call-done, s32[1024]{0:T(1024)S(1)} %pad_clamp_fusion), kind=kCustom, calls=%fused_computation.4 | custom fusion | bytes 25166848 | tf_op jit(solution)/shard_map/jit(_take)/gather | solution.py:21
  1107.1 27.1 %copy.34 = bf16[4,2,32,128,192]{4,2,3,0,1:T(8,128)(2,1)} copy(bf16[4,2,32,128,192]{3,4,2,1,0:T(8,128)(2,1)} %bitcast.364) | data formatting | bytes 25165824 | tf_op jit(solution)/shard_map/jit(_take)/gather | solution.py:21
  1134.2 14.1 %broadcast_select_fusion = bf16[4,2,32,128,192]{4,2,3,0,1:T(8,128)(2,1)} fusion(bf16[4,2,32,128,192]{4,2,3,0,1:T(8,128)(2,1)} %copy.34, pred[4,2,32]{2,0,1:T(4,128)(4,1)S(1)} %copy.28), kind=kLoop, calls=%fused_computation.5 | loop fusion | flops 6291456 | bytes 25166080 | tf_op jit(solution)/shard_map/jit(_take)/select_n | solution.py:21
  1148.4 11.3 broadcast_multiply_fusion
  1159.7 11.9 fusion.6
  1171.6 6.1 convolution_bitcast_fusion
  1177.7 0.7 dynamic_slice.7
  1178.4 32.5 %reduce-scatter.2.cloned.1.call-done = f32[1024,128]{0,1:T(8,128)} async-done(((f32[4096,128]{0,1:T(8,128)}), f32[1024,128]{0,1:T(8,128)}) %reduce-scatter.2.cloned.1.call-update) | async-done | bytes 524304 | tf_op jit(solution)/shard_map/reduce_scatter | solution.py:62
  1210.9 1.2 add_reduce_fusion
  1212.1 8.6 all-reduce
  1220.7 2.0 fusion.9
  (94 shorter events, 4.8 us)
Async XLA Ops:
  6.5 1153.2 %copy-start = (bf16[4,32,8]{1,2,0:T(8,128)(2,1)S(1)}, bf16[4,32,8]{1,2,0:T(8,128)(2,1)}, u32[]{:S(2)}) copy-start(bf16[4,32,8]{1,2,0:T(8,128)(2,1)} %param.14) | copy-start | bytes 6148
  6.5 1081.8 %all-gather.2.cloned.1.call-start = ((), (), s32[]{:S(2)}) async-start(), calls=%async_computation.2 | async-start | bytes 31457280 | tf_op jit(solution)/shard_map/all_gather | solution.py:55
  687.1 10.1 copy-start.1
  863.3 0.7 copy-start.3
  863.3 347.6 %reduce-scatter.2.cloned.1.call-start = ((), (), s32[]{:S(2)}) async-start(), calls=%async_computation.3 | async-start | bytes 2621440 | tf_op jit(solution)/shard_map/reduce_scatter | solution.py:62
  1171.6 49.1 %copy-start.2 = (f32[1024]{0:T(1024)S(1)}, f32[1024]{0:T(1024)}, u32[]{:S(2)}) copy-start(f32[1024]{0:T(1024)} %param.17) | copy-start | bytes 12292
Sparse Core Ops, SparseCore 0:
  863.4 224.8 all-gather.1
  1177.8 33.0 reduce-scatter.1
